TPU v7x, 256 devices: a whole 4x4x8 slice. The times are simulated.
256 devices in a mesh: grp: 8 (over x, core), lat: 32 (over z, y).
Axes of the slice: x: 4, y: 4, z: 8, core: 2. Of those that a mesh axis runs over, the one named last changes fastest.
Arguments:
- coefficients: bfloat16 [192, 12288, 256], P('grp', 'lat'), may hold values from -6 to 6
- leaf: bfloat16 [192, 4096, 384], P('grp', 'lat'), may hold values from -0.3125 to 0.3125
- mix_self: bfloat16 [192, 5, 4096, 128], P('grp', None, 'lat'), may hold values from -0.375 to 0.375
- mix_partner: bfloat16 [192, 5, 2048, 128], P('grp', None, 'lat'), may hold values from -0.5 to 0.5
- skeleton: int32 [192, 5, 2048], P('grp', None, 'lat'), may hold values from 0 to 127, as said below
- expand: bfloat16 [192, 2048, 128], P('grp', 'lat'), may hold values from -0.5 to 0.5
- slot_order: int32 [192], replicated, may hold values from -1 to 143, as said below
Outputs:
- field: bfloat16 [256, 2048, 128], P('grp', 'lat')
Inputs may be any that keep to these rules, and one draw needn't show every extreme that they name: `slot_order`: each order 0 to 143 stands in exactly one slot, all other slots hold -1; in every draw some group of 24 slots is full. `skeleton`: for each slot, level and block the 64 indices are distinct.
All inputs are finite; a program needn't handle non-finite values.
Results may differ from a plain program's by a relative error of at most 0.012.
Values may be sent and summed in bfloat16 or wider, within the bound.
A program may use at most 64 MiB of HBM per device.

v0:
```python
import math

import jax
import jax.numpy as jnp
from jax import lax
from jax.sharding import PartitionSpec as P

LON_DEV = 32


def swapped(value, axis, distance):
    mask = 2**distance
    pairs = [(source, source ^ mask) for source in range(lax.axis_size(axis))]
    return lax.ppermute(value, axis, pairs)


def selector(wanted, width):
    column = jnp.arange(width, dtype=jnp.int32)
    return (wanted[:, :, None] == column[None, None, :]).astype(jnp.bfloat16)


def trig_tables(orders, lon_start, lon_count, lon_total, scale):
    column = lon_start + jnp.arange(lon_count, dtype=jnp.int32)
    live = orders >= 0
    degree = jnp.maximum(orders, 0)
    remain = degree[:, None] * column[None, :] % lon_total
    angle = 2.0 * math.pi * remain.astype(jnp.float32) / lon_total
    cos_table = jnp.where(live[:, None], jnp.cos(angle) * scale, 0.0).astype(jnp.bfloat16)
    sin_table = jnp.where(live[:, None], -jnp.sin(angle) * scale, 0.0).astype(jnp.bfloat16)
    return (cos_table, sin_table)


def synthesize(fields, orders, lon_start, lon_count, lon_total, scale):
    cos_table, sin_table = trig_tables(orders, lon_start, lon_count, lon_total, scale)
    half = fields.shape[2] // 2
    total = jnp.einsum(
        "kls,kj->jls", fields[:, :, :half], cos_table, preferred_element_type=jnp.float32
    )
    return total + jnp.einsum(
        "kls,kj->jls", fields[:, :, half:], sin_table, preferred_element_type=jnp.float32
    )


def on_device(coefficients, leaf, mix_self, mix_partner, skeleton, expand, slot_order):
    slot_count = coefficients.shape[0]
    width = leaf.shape[1]
    state = jnp.einsum(
        "kad,kds->kas", leaf, coefficients, preferred_element_type=jnp.float32
    ).astype(jnp.bfloat16)
    levels = lax.axis_size("lat").bit_length() - 1
    for level in range(levels):
        wanted = skeleton[:, level, :]
        mixed = jnp.einsum(
            "kac,kcs->kas", mix_self[:, level], state, preferred_element_type=jnp.float32
        )
        asked = swapped(wanted, "lat", level)
        chosen = jnp.einsum(
            "krc,kcs->krs", selector(asked, width), state, preferred_element_type=jnp.float32
        ).astype(jnp.bfloat16)
        picked = swapped(chosen, "lat", level)
        mixed = mixed + jnp.einsum(
            "kra,krs->kas", mix_partner[:, level], picked, preferred_element_type=jnp.float32
        )
        state = mixed.astype(jnp.bfloat16)
    fields = jnp.einsum("kla,kas->kls", expand, state, preferred_element_type=jnp.float32).astype(
        jnp.bfloat16
    )
    groups = lax.axis_size("grp")
    lon_total = LON_DEV * groups
    scale = 1.0 / math.sqrt(groups * slot_count * 3 // 4)
    pieces = lax.all_to_all(fields, "grp", split_axis=1, concat_axis=0, tiled=True)
    whole = synthesize(pieces, slot_order, 0, lon_total, lon_total, scale).astype(jnp.bfloat16)
    return lax.all_to_all(whole, "grp", split_axis=0, concat_axis=1, tiled=True)


def solution(mesh):
    return jax.shard_map(
        on_device,
        mesh=mesh,
        in_specs=(
            P("grp", "lat", None),
            P("grp", "lat", None),
            P("grp", None, "lat", None),
            P("grp", None, "lat", None),
            P("grp", None, "lat"),
            P("grp", "lat", None),
            P(),
        ),
        out_specs=P("grp", "lat", None),
        check_vma=False,
    )
```

profile of v0, /device:TPU:1, one launch (start us, length us, event | category | flops | bytes accessed | tf_op | source)
XLA Modules:
  0.0 186.0 jit_solution(17816442994996431904)
XLA Ops:
  0.9 2.1 %collective-permute-start = (s32[24,64]{1,0:T(8,128)S(1)}, s32[24,64]{1,0:T(8,128)S(1)}, u32[]{:S(2)}, u32[]{:S(2)}) collective-permute-start(s32[24,64]{1,0:T(8,128)S(1)} %get-tuple-element.8), channel_id=1, source_target_pairs={{0,1},{1,0},{2,3},{3,2},{4,5},{5,4},{6,7},{7,6},{8,9},{9,8},{10,11... | collective-permute-start | bytes 18440 | tf_op jit(solution)/shard_map/ppermute | solution.py:14
  3.0 3.5 %convolution_convert_fusion = bf16[24,128,256]{2,1,0:T(8,128)(2,1)S(1)} fusion(bf16[24,128,384]{2,1,0:T(8,128)(2,1)S(1)} %copy-done, bf16[24,384,256]{2,1,0:T(8,128)(2,1)} %param.7), kind=kOutput, calls=%fused_computation.5 | convolution fusion | flops 604766208 | bytes 8650752 | tf_op jit(solution)/shard_map/kad,kds->kas/dot_general | solution.py:47
  7.9 2.6 %collective-permute-start.2 = (s32[24,64]{1,0:T(8,128)S(1)}, s32[24,64]{1,0:T(8,128)S(1)}, u32[]{:S(2)}, u32[]{:S(2)}) collective-permute-start(s32[24,64]{1,0:T(8,128)S(1)} %get-tuple-element.7), channel_id=1, source_target_pairs={{0,2},{1,3},{2,0},{3,1},{4,6},{5,7},{6,4},{7,5},{8,10},{9,11},{10,... | collective-permute-start | bytes 18440 | tf_op jit(solution)/shard_map/ppermute | solution.py:14
  11.1 13.1 %collective-permute-done.1 = bf16[24,64,256]{2,1,0:T(8,128)(2,1)S(1)} collective-permute-done((bf16[24,64,256]{2,1,0:T(8,128)(2,1)S(1)}, bf16[24,64,256]{2,1,0:T(8,128)(2,1)S(1)}, u32[]{:S(2)}, u32[]{:S(2)}) %collective-permute-start.1) | collective-permute-done | bytes 786464 | tf_op jit(solution)/shard_map/ppermute | solution.py:14
  24.9 2.5 %collective-permute-done.2 = s32[24,64]{1,0:T(8,128)S(1)} collective-permute-done((s32[24,64]{1,0:T(8,128)S(1)}, s32[24,64]{1,0:T(8,128)S(1)}, u32[]{:S(2)}, u32[]{:S(2)}) %collective-permute-start.2) | collective-permute-done | bytes 6176 | tf_op jit(solution)/shard_map/ppermute | solution.py:14
  28.1 1.2 collective-permute-start.3
  29.3 1.6 collective-permute-start.4
  31.5 15.5 %collective-permute-done.3 = bf16[24,64,256]{2,1,0:T(8,128)(2,1)S(1)} collective-permute-done((bf16[24,64,256]{2,1,0:T(8,128)(2,1)S(1)}, bf16[24,64,256]{2,1,0:T(8,128)(2,1)S(1)}, u32[]{:S(2)}, u32[]{:S(2)}) %collective-permute-start.3) | collective-permute-done | bytes 786464 | tf_op jit(solution)/shard_map/ppermute | solution.py:14
  48.4 1.7 collective-permute-start.5
  50.1 3.0 %collective-permute-start.6 = (s32[24,64]{1,0:T(8,128)S(1)}, s32[24,64]{1,0:T(8,128)S(1)}, u32[]{:S(2)}, u32[]{:S(2)}) collective-permute-start(s32[24,64]{1,0:T(8,128)S(1)} %get-tuple-element.9), channel_id=1, source_target_pairs={{0,8},{1,9},{2,10},{3,11},{4,12},{5,13},{6,14},{7,15},{8,0},{9,1},... | collective-permute-start | bytes 18440 | tf_op jit(solution)/shard_map/ppermute | solution.py:14
  53.7 11.8 %collective-permute-done.5 = bf16[24,64,256]{2,1,0:T(8,128)(2,1)S(1)} collective-permute-done((bf16[24,64,256]{2,1,0:T(8,128)(2,1)S(1)}, bf16[24,64,256]{2,1,0:T(8,128)(2,1)S(1)}, u32[]{:S(2)}, u32[]{:S(2)}) %collective-permute-start.5) | collective-permute-done | bytes 786464 | tf_op jit(solution)/shard_map/ppermute | solution.py:14
  66.9 2.8 %collective-permute-start.7 = (bf16[24,64,256]{2,1,0:T(8,128)(2,1)S(1)}, bf16[24,64,256]{2,1,0:T(8,128)(2,1)S(1)}, u32[]{:S(2)}, u32[]{:S(2)}) collective-permute-start(bf16[24,64,256]{2,1,0:T(8,128)(2,1)S(1)} %convolution_convert_fusion.2), channel_id=1, source_target_pairs={{0,8},{1,9},{2,10},{3,11},{4,12},{5,13},{6,14},{7,15},{8,0},{9,1},... | collective-permute-start | bytes 2359304 | tf_op jit(solution)/shard_map/ppermute | solution.py:14
  69.7 4.8 %collective-permute-start.8 = (s32[24,64]{1,0:T(8,128)S(1)}, s32[24,64]{1,0:T(8,128)S(1)}, u32[]{:S(2)}, u32[]{:S(2)}) collective-permute-start(s32[24,64]{1,0:T(8,128)S(1)} %get-tuple-element.5), channel_id=1, source_target_pairs={{0,16},{1,17},{2,18},{3,19},{4,20},{5,21},{6,22},{7,23},{8,24},{9,... | collective-permute-start | bytes 18440 | tf_op jit(solution)/shard_map/ppermute | solution.py:14
  75.0 28.9 %collective-permute-done.7 = bf16[24,64,256]{2,1,0:T(8,128)(2,1)S(1)} collective-permute-done((bf16[24,64,256]{2,1,0:T(8,128)(2,1)S(1)}, bf16[24,64,256]{2,1,0:T(8,128)(2,1)S(1)}, u32[]{:S(2)}, u32[]{:S(2)}) %collective-permute-start.7) | collective-permute-done | bytes 786464 | tf_op jit(solution)/shard_map/ppermute | solution.py:14
  105.3 7.5 %collective-permute-start.9 = (bf16[24,64,256]{2,1,0:T(8,128)(2,1)S(1)}, bf16[24,64,256]{2,1,0:T(8,128)(2,1)}, u32[]{:S(2)}, u32[]{:S(2)}) collective-permute-start(bf16[24,64,256]{2,1,0:T(8,128)(2,1)S(1)} %convolution_convert_fusion.1), channel_id=1, source_target_pairs={{0,16},{1,17},{2,18},{3,19},{4,20},{5,21},{6,22},{7,23},{8,24},{9,... | collective-permute-start | bytes 2359304 | tf_op jit(solution)/shard_map/ppermute | solution.py:14
  112.8 2.2 %fusion.12 = f32[24,256,128]{2,1,0:T(8,128)} fusion(bf16[24,256,128]{2,1,0:T(8,128)(2,1)S(1)} %add_convert_fusion.1, bf16[24,5,128,128]{3,2,1,0:T(8,128)(2,1)S(1)} %copy-done.1), kind=kOutput, calls=%fused_computation.24 | convolution fusion | flops 201326592 | bytes 5505024 | tf_op jit(solution)/shard_map/kac,kcs->kas/dot_general | solution.py:53
  115.0 32.4 %collective-permute-done.9 = bf16[24,64,256]{2,1,0:T(8,128)(2,1)} collective-permute-done((bf16[24,64,256]{2,1,0:T(8,128)(2,1)S(1)}, bf16[24,64,256]{2,1,0:T(8,128)(2,1)}, u32[]{:S(2)}, u32[]{:S(2)}) %collective-permute-start.9) | collective-permute-done | bytes 786464 | tf_op jit(solution)/shard_map/ppermute | solution.py:14
  147.4 3.4 %fusion.2 = bf16[24,64,256]{2,1,0:T(8,128)(2,1)S(1)} fusion(bf16[24,64,128]{2,1,0:T(8,128)(2,1)S(1)} %copy-done.3, f32[24,256,128]{2,1,0:T(8,128)} %fusion.12, bf16[24,64,256]{2,1,0:T(8,128)(2,1)} %collective-permute-done.9, bf16[24,5,64,128]{3,2,1,0:T(8,128)(2,1)} %param.10), kind=kOutput, calls=%fused_computation.14 | convolution fusion | flops 203292672 | bytes 5505024 | tf_op jit(solution)/shard_map/kla,kas->kls/dot_general | solution.py:65
  150.8 1.3 copy.28
  152.2 5.5 %all-to-all-start = ((bf16[24,64,256]{2,0,1:T(8,128)(2,1)}), bf16[24,64,256]{2,0,1:T(8,128)(2,1)S(1)}, u32[]{:S(2)}, u32[]{:S(2)}) async-start(bf16[24,64,256]{2,0,1:T(8,128)(2,1)} %copy.28), calls=%async_computation | async-start | bytes 1572864 | tf_op jit(solution)/shard_map/all_to_all | solution.py:71
  157.6 12.1 %all-to-all-done = bf16[24,64,256]{2,0,1:T(8,128)(2,1)S(1)} async-done(((bf16[24,64,256]{2,0,1:T(8,128)(2,1)}), bf16[24,64,256]{2,0,1:T(8,128)(2,1)S(1)}, u32[]{:S(2)}, u32[]{:S(2)}) %all-to-all-start) | async-done | bytes 786464 | tf_op jit(solution)/shard_map/all_to_all | solution.py:71
  169.8 1.1 fusion.20
  170.9 1.1 fusion.3
  172.4 12.7 %all_to_all.36 = bf16[256,8,128]{2,1,0:T(8,128)(2,1)S(1)} all-to-all(bf16[256,8,128]{2,1,0:T(8,128)(2,1)S(1)} %copy.30), channel_id=1, replica_groups=mesh['grp'=8,'lat'=32] {'grp'}, dimensions={0} | all-to-all | bytes 1048576 | tf_op jit(solution)/shard_map/all_to_all | solution.py:73
  (34 shorter events, 11.4 us)
Async XLA Ops:
  0.0 3.0 %copy-start = (bf16[24,128,384]{2,1,0:T(8,128)(2,1)S(1)}, bf16[24,128,384]{2,1,0:T(8,128)(2,1)}, u32[]{:S(2)}) copy-start(bf16[24,128,384]{2,1,0:T(8,128)(2,1)} %param.8) | copy-start | bytes 7077892
  0.9 5.6 %collective-permute-start = (s32[24,64]{1,0:T(8,128)S(1)}, s32[24,64]{1,0:T(8,128)S(1)}, u32[]{:S(2)}, u32[]{:S(2)}) collective-permute-start(s32[24,64]{1,0:T(8,128)S(1)} %get-tuple-element.8), channel_id=1, source_target_pairs={{0,1},{1,0},{2,3},{3,2},{4,5},{5,4},{6,7},{7,6},{8,9},{9,8},{10,11... | collective-permute-start | bytes 18440 | tf_op jit(solution)/shard_map/ppermute | solution.py:14
  3.0 7.5 %copy-start.1 = (bf16[24,5,128,128]{3,2,1,0:T(8,128)(2,1)S(1)}, bf16[24,5,128,128]{3,2,1,0:T(8,128)(2,1)}, u32[]{:S(2)}) copy-start(bf16[24,5,128,128]{3,2,1,0:T(8,128)(2,1)} %param.9) | copy-start | bytes 11796484
  7.0 17.3 %collective-permute-start.1 = (bf16[24,64,256]{2,1,0:T(8,128)(2,1)S(1)}, bf16[24,64,256]{2,1,0:T(8,128)(2,1)S(1)}, u32[]{:S(2)}, u32[]{:S(2)}) collective-permute-start(bf16[24,64,256]{2,1,0:T(8,128)(2,1)S(1)} %convolution_convert_fusion.5), channel_id=1, source_target_pairs={{0,1},{1,0},{2,3},{3,2},{4,5},{5,4},{6,7},{7,6},{8,9},{9,8},{10,11... | collective-permute-start | bytes 2359304 | tf_op jit(solution)/shard_map/ppermute | solution.py:14
  7.9 16.4 %copy-start.2 = (bf16[24,5,64,128]{3,2,1,0:T(8,128)(2,1)S(1)}, bf16[24,5,64,128]{3,2,1,0:T(8,128)(2,1)}, u32[]{:S(2)}) copy-start(bf16[24,5,64,128]{3,2,1,0:T(8,128)(2,1)} %param.10) | copy-start | bytes 5898244
  7.9 19.5 %collective-permute-start.2 = (s32[24,64]{1,0:T(8,128)S(1)}, s32[24,64]{1,0:T(8,128)S(1)}, u32[]{:S(2)}, u32[]{:S(2)}) collective-permute-start(s32[24,64]{1,0:T(8,128)S(1)} %get-tuple-element.7), channel_id=1, source_target_pairs={{0,2},{1,3},{2,0},{3,1},{4,6},{5,7},{6,4},{7,5},{8,10},{9,11},{10,... | collective-permute-start | bytes 18440 | tf_op jit(solution)/shard_map/ppermute | solution.py:14
  28.1 18.9 %collective-permute-start.3 = (bf16[24,64,256]{2,1,0:T(8,128)(2,1)S(1)}, bf16[24,64,256]{2,1,0:T(8,128)(2,1)S(1)}, u32[]{:S(2)}, u32[]{:S(2)}) collective-permute-start(bf16[24,64,256]{2,1,0:T(8,128)(2,1)S(1)} %convolution_convert_fusion.4), channel_id=1, source_target_pairs={{0,2},{1,3},{2,0},{3,1},{4,6},{5,7},{6,4},{7,5},{8,10},{9,11},{10,... | collective-permute-start | bytes 2359304 | tf_op jit(solution)/shard_map/ppermute | solution.py:14
  29.3 18.3 %collective-permute-start.4 = (s32[24,64]{1,0:T(8,128)S(1)}, s32[24,64]{1,0:T(8,128)S(1)}, u32[]{:S(2)}, u32[]{:S(2)}) collective-permute-start(s32[24,64]{1,0:T(8,128)S(1)} %get-tuple-element.6), channel_id=1, source_target_pairs={{0,4},{1,5},{2,6},{3,7},{4,0},{5,1},{6,2},{7,3},{8,12},{9,13},{10,... | collective-permute-start | bytes 18440 | tf_op jit(solution)/shard_map/ppermute | solution.py:14
  48.4 17.1 %collective-permute-start.5 = (bf16[24,64,256]{2,1,0:T(8,128)(2,1)S(1)}, bf16[24,64,256]{2,1,0:T(8,128)(2,1)S(1)}, u32[]{:S(2)}, u32[]{:S(2)}) collective-permute-start(bf16[24,64,256]{2,1,0:T(8,128)(2,1)S(1)} %convolution_convert_fusion.3), channel_id=1, source_target_pairs={{0,4},{1,5},{2,6},{3,7},{4,0},{5,1},{6,2},{7,3},{8,12},{9,13},{10,... | collective-permute-start | bytes 2359304 | tf_op jit(solution)/shard_map/ppermute | solution.py:14
  50.1 16.1 %collective-permute-start.6 = (s32[24,64]{1,0:T(8,128)S(1)}, s32[24,64]{1,0:T(8,128)S(1)}, u32[]{:S(2)}, u32[]{:S(2)}) collective-permute-start(s32[24,64]{1,0:T(8,128)S(1)} %get-tuple-element.9), channel_id=1, source_target_pairs={{0,8},{1,9},{2,10},{3,11},{4,12},{5,13},{6,14},{7,15},{8,0},{9,1},... | collective-permute-start | bytes 18440 | tf_op jit(solution)/shard_map/ppermute | solution.py:14
  66.9 37.1 %collective-permute-start.7 = (bf16[24,64,256]{2,1,0:T(8,128)(2,1)S(1)}, bf16[24,64,256]{2,1,0:T(8,128)(2,1)S(1)}, u32[]{:S(2)}, u32[]{:S(2)}) collective-permute-start(bf16[24,64,256]{2,1,0:T(8,128)(2,1)S(1)} %convolution_convert_fusion.2), channel_id=1, source_target_pairs={{0,8},{1,9},{2,10},{3,11},{4,12},{5,13},{6,14},{7,15},{8,0},{9,1},... | collective-permute-start | bytes 2359304 | tf_op jit(solution)/shard_map/ppermute | solution.py:14
  69.7 34.9 %collective-permute-start.8 = (s32[24,64]{1,0:T(8,128)S(1)}, s32[24,64]{1,0:T(8,128)S(1)}, u32[]{:S(2)}, u32[]{:S(2)}) collective-permute-start(s32[24,64]{1,0:T(8,128)S(1)} %get-tuple-element.5), channel_id=1, source_target_pairs={{0,16},{1,17},{2,18},{3,19},{4,20},{5,21},{6,22},{7,23},{8,24},{9,... | collective-permute-start | bytes 18440 | tf_op jit(solution)/shard_map/ppermute | solution.py:14
  105.3 42.1 %copy-start.3 = (bf16[24,64,128]{2,1,0:T(8,128)(2,1)S(1)}, bf16[24,64,128]{2,1,0:T(8,128)(2,1)}, u32[]{:S(2)}) copy-start(bf16[24,64,128]{2,1,0:T(8,128)(2,1)} %param.12) | copy-start | bytes 1179652
  105.3 42.1 %collective-permute-start.9 = (bf16[24,64,256]{2,1,0:T(8,128)(2,1)S(1)}, bf16[24,64,256]{2,1,0:T(8,128)(2,1)}, u32[]{:S(2)}, u32[]{:S(2)}) collective-permute-start(bf16[24,64,256]{2,1,0:T(8,128)(2,1)S(1)} %convolution_convert_fusion.1), channel_id=1, source_target_pairs={{0,16},{1,17},{2,18},{3,19},{4,20},{5,21},{6,22},{7,23},{8,24},{9,... | collective-permute-start | bytes 2359304 | tf_op jit(solution)/shard_map/ppermute | solution.py:14
  150.8 6.8 %copy-start.4 = (s32[192]{0:T(256)S(1)}, s32[192]{0:T(256)}, u32[]{:S(2)}) copy-start(s32[192]{0:T(256)} %param.13) | copy-start | bytes 2308
  152.2 17.6 %all-to-all-start = ((bf16[24,64,256]{2,0,1:T(8,128)(2,1)}), bf16[24,64,256]{2,0,1:T(8,128)(2,1)S(1)}, u32[]{:S(2)}, u32[]{:S(2)}) async-start(bf16[24,64,256]{2,0,1:T(8,128)(2,1)} %copy.28), calls=%async_computation | async-start | bytes 1572864 | tf_op jit(solution)/shard_map/all_to_all | solution.py:71
where the time goes:
time: 186 us
  waiting for transfers between devices  116 us (62%)
  starting transfers between devices  33.7 us (18%)
  matrix products  19.5 us (10%)
  blocking collectives  12.7 us (7%)
  local copies, waits for them, and re-layouts  3.61 us (2%)
    ppermute x10, waiting for transfers between devices, swapped(): return lax.ppermute(value, axis, pairs)  104 us
    ppermute x10, starting transfers between devices, swapped(): return lax.ppermute(value, axis, pairs)  28.2 us
    all_to_all x1, blocking collectives, on_device(): return lax.all_to_all(whole, 'grp', split_axis=0, concat_axis=1, tiled=True)  12.7 us
    all_to_all x1, waiting for transfers between devices, on_device(): lax.all_to_all(fields, 'grp', split_axis=1, concat_axis=0, tiled=True)  12.1 us
    all_to_all x1, starting transfers between devices, on_device(): lax.all_to_all(fields, 'grp', split_axis=1, concat_axis=0, tiled=True)  5.46 us
    dot_general x5, matrix products, on_device(): jnp.einsum('kac,kcs->kas', mix_self[:, level], state, preferred_element_t...  4.58 us
  transfers between devices with their start and end apart: 11, of which 7 were waited for; matrix products, arithmetic and copies ran while one was open for 6% of the time, Pallas kernels for 0%

commit v1 on v0

v1 whole, which is shorter than its diff:
```python
import functools
import math

import jax
import jax.numpy as jnp
from jax import lax
from jax.experimental import pallas as pl
from jax.experimental.pallas import tpu as pltpu
from jax.sharding import PartitionSpec as P

LON_DEV = 32
GROUP = 3
MESH = pl.DeviceIdType.MESH
F32 = jnp.float32
BF16 = jnp.bfloat16


def dot(a, b):
    return jnp.dot(a, b, preferred_element_type=F32)


def dot_rows(a, b):
    return lax.dot_general(a, b, (((0,), (0,)), ((), ())), preferred_element_type=F32)


def kernel(
    levels, groups, gsize,
    coeff_h, leaf_h, self_h, partner_h, skel_ref, expand_h, order_ref, out_h,
    coeff_v, leaf_v, self_v, partner_v, expand_v,
    ask_send, ask_recv, state, send_v, recv_v,
    fields, pieces, pieces_w, whole_w, whole,
    in_sem, ask_ssem, ask_rsem, ssem, rsem, fssem, frsem, ossem, orsem, own_sem,
):
    slots, width = state.shape[0], state.shape[1]
    half = coeff_v.shape[2] // 2
    chunks = slots // gsize
    lat_part = fields.shape[2]
    grp = lax.axis_index("grp")
    lat = lax.axis_index("lat")
    partners = []
    for k in range(levels):
        mask = 2**k
        partners.append(lat + (1 - 2 * ((lat // mask) % 2)) * mask)
    others = [(grp + d) % groups for d in range(1, groups)]
    senders = [(grp + groups - d) % groups for d in range(1, groups)]

    def span(c):
        return pl.ds(c * gsize, gsize)

    loads = (
        (coeff_h, coeff_v), (leaf_h, leaf_v), (self_h, self_v),
        (partner_h, partner_v), (expand_h, expand_v),
    )

    def load(i, c):
        source, target = loads[i]
        return pltpu.make_async_copy(source.at[span(c)], target.at[span(c)], in_sem.at[i, c])

    def start_loads(c, _):
        for i in range(len(loads)):
            load(i, c).start()
        return 0

    lax.fori_loop(0, chunks, start_loads, 0)

    barrier = pltpu.get_barrier_semaphore()
    for k in range(levels):
        pl.semaphore_signal(barrier, inc=1, device_id={"lat": partners[k]}, device_id_type=MESH)
    for other in others:
        pl.semaphore_signal(barrier, inc=1, device_id={"grp": other}, device_id_type=MESH)
    for k in range(levels):
        ask_send[k] = skel_ref[:, k, :]
    pl.semaphore_wait(barrier, levels + groups - 1)

    def ask(k):
        return pltpu.make_async_remote_copy(
            src_ref=ask_send.at[k], dst_ref=ask_recv.at[k],
            send_sem=ask_ssem.at[k], recv_sem=ask_rsem.at[k],
            device_id={"lat": partners[k]}, device_id_type=MESH,
        )

    for k in range(levels):
        ask(k).start()

    def exchange(k, c):
        return pltpu.make_async_remote_copy(
            src_ref=send_v.at[k, span(c)], dst_ref=recv_v.at[k, span(c)],
            send_sem=ssem.at[k], recv_sem=rsem.at[k, c],
            device_id={"lat": partners[k]}, device_id_type=MESH,
        )

    def hand_over(d, c):
        return pltpu.make_async_remote_copy(
            src_ref=fields.at[others[d], span(c)], dst_ref=pieces.at[grp, span(c)],
            send_sem=fssem.at[d], recv_sem=frsem.at[d],
            device_id={"grp": others[d]}, device_id_type=MESH,
        )

    row_of = lax.broadcasted_iota(jnp.int32, (width, ask_recv.shape[2]), 0)

    def stage(k, c):
        if k == 0:
            load(0, c).wait()
            load(1, c).wait()
        else:
            if k == 1:
                load(2, c).wait()
                load(3, c).wait()
            if k == levels:
                load(4, c).wait()
            exchange(k - 1, c).wait_recv()
        for i in range(gsize):
            q = c * gsize + i
            if k == 0:
                now = dot(leaf_v[q], coeff_v[q]).astype(BF16)
            else:
                mixed = dot(self_v[q, k - 1], state[q])
                mixed = mixed + dot_rows(partner_v[q, k - 1], recv_v[k - 1, q])
                now = mixed.astype(BF16)
            if k < levels:
                wanted = ask_recv[k, pl.ds(q, 1), :]
                pick = (row_of == wanted).astype(F32).astype(BF16)
                send_v[k, q] = dot_rows(pick, now).astype(BF16)
                state[q] = now
            else:
                field = dot(expand_v[q], now).astype(BF16)
                for g in range(groups):
                    fields[g, q] = field[g * lat_part:(g + 1) * lat_part]
        if k < levels:
            exchange(k, c).start()
        else:
            for d in range(groups - 1):
                hand_over(d, c).start()

    def step(t, _):
        for k in range(levels + 1):
            c = t - k

            @pl.when((c >= 0) & (c < chunks))
            def _():
                if k < levels:
                    @pl.when(c == 0)
                    def _():
                        ask(k).wait_recv()

                stage(k, c)
        return 0

    lax.fori_loop(0, chunks + levels, step, 0)

    lons = whole.shape[0]
    total = groups * slots
    order = order_ref[...]
    turn = lax.broadcasted_iota(jnp.int32, (lons, total), 0)
    turn = (jnp.maximum(order, 0) * turn) % lons
    angle = 2.0 * math.pi * turn.astype(F32) / lons
    scale = jnp.where(order >= 0, 1.0 / math.sqrt(total * 3 // 4), 0.0)
    cos_table = (jnp.cos(angle) * scale).astype(BF16)
    sin_table = (-jnp.sin(angle) * scale).astype(BF16)

    pieces_w[pl.ds(grp * slots, slots)] = fields[grp].astype(F32)
    for d in range(groups - 1):
        pltpu.make_async_remote_copy(
            src_ref=fields.at[others[d]], dst_ref=pieces.at[senders[d]],
            send_sem=fssem.at[d], recv_sem=frsem.at[d],
            device_id={"grp": others[d]}, device_id_type=MESH,
        ).wait_recv()
        pieces_w[pl.ds(senders[d] * slots, slots)] = pieces[senders[d]].astype(F32)

    for row in range(0, lat_part, 2):
        cos_part, sin_part = [], []
        for at in (row, row + 1):
            cos_part.append(pieces_w[:, at, :half])
            sin_part.append(pieces_w[:, at, half:])
        mapped = dot(cos_table, jnp.concatenate(cos_part, axis=1).astype(BF16))
        mapped = mapped + dot(sin_table, jnp.concatenate(sin_part, axis=1).astype(BF16))
        whole_w[:, row, :] = mapped[:, :half]
        whole_w[:, row + 1, :] = mapped[:, half:]
    whole[...] = whole_w[...].astype(BF16)

    lon_dev = lons // groups

    def scatter(d):
        return pltpu.make_async_remote_copy(
            src_ref=whole.at[pl.ds(others[d] * lon_dev, lon_dev)],
            dst_ref=out_h.at[:, pl.ds(grp * lat_part, lat_part), :],
            send_sem=ossem.at[d], recv_sem=orsem.at[d],
            device_id={"grp": others[d]}, device_id_type=MESH,
        )

    for d in range(groups - 1):
        scatter(d).start()
    own = pltpu.make_async_copy(
        whole.at[pl.ds(grp * lon_dev, lon_dev)],
        out_h.at[:, pl.ds(grp * lat_part, lat_part), :], own_sem,
    )
    own.start()
    own.wait()
    for k in range(levels):
        ask(k).wait_send()
        pltpu.make_async_remote_copy(
            src_ref=send_v.at[k], dst_ref=recv_v.at[k],
            send_sem=ssem.at[k], recv_sem=rsem.at[k, 0],
            device_id={"lat": partners[k]}, device_id_type=MESH,
        ).wait_send()
    for d in range(groups - 1):
        pltpu.make_async_remote_copy(
            src_ref=fields.at[others[d]], dst_ref=pieces.at[grp],
            send_sem=fssem.at[d], recv_sem=frsem.at[d],
            device_id={"grp": others[d]}, device_id_type=MESH,
        ).wait_send()
        scatter(d).wait_send()
        pltpu.make_async_remote_copy(
            src_ref=whole.at[pl.ds(others[d] * lon_dev, lon_dev)],
            dst_ref=out_h.at[:, pl.ds(senders[d] * lat_part, lat_part), :],
            send_sem=ossem.at[d], recv_sem=orsem.at[d],
            device_id={"grp": others[d]}, device_id_type=MESH,
        ).wait_recv()


def on_device(coefficients, leaf, mix_self, mix_partner, skeleton, expand, slot_order):
    slots, _, columns = coefficients.shape
    width = leaf.shape[1]
    rank = mix_partner.shape[2]
    lats = expand.shape[1]
    levels = lax.axis_size("lat").bit_length() - 1
    groups = lax.axis_size("grp")
    lons = LON_DEV * groups
    half = columns // 2
    part = lats // groups
    chunks = slots // GROUP
    dma = pltpu.SemaphoreType.DMA
    anywhere = pl.BlockSpec(memory_space=pl.ANY)
    vmem = pl.BlockSpec(memory_space=pltpu.VMEM)
    return pl.pallas_call(
        functools.partial(kernel, levels, groups, GROUP),
        out_shape=jax.ShapeDtypeStruct((LON_DEV, lats, half), BF16),
        in_specs=[anywhere, anywhere, anywhere, anywhere, vmem, anywhere, vmem],
        out_specs=anywhere,
        scratch_shapes=[
            pltpu.VMEM(coefficients.shape, BF16),
            pltpu.VMEM(leaf.shape, BF16),
            pltpu.VMEM(mix_self.shape, BF16),
            pltpu.VMEM(mix_partner.shape, BF16),
            pltpu.VMEM(expand.shape, BF16),
            pltpu.VMEM((levels, slots, rank), jnp.int32),
            pltpu.VMEM((levels, slots, rank), jnp.int32),
            pltpu.VMEM((slots, width, columns), BF16),
            pltpu.VMEM((levels, slots, rank, columns), BF16),
            pltpu.VMEM((levels, slots, rank, columns), BF16),
            pltpu.VMEM((groups, slots, part, columns), BF16),
            pltpu.VMEM((groups, slots, part, columns), BF16),
            pltpu.VMEM((groups * slots, part, columns), F32),
            pltpu.VMEM((lons, part, half), F32),
            pltpu.VMEM((lons, part, half), BF16),
            dma((5, chunks)),
            dma((levels,)), dma((levels,)),
            dma((levels,)), dma((levels, chunks)),
            dma((groups - 1,)), dma((groups - 1,)),
            dma((groups - 1,)), dma((groups - 1,)),
            dma,
        ],
        compiler_params=pltpu.CompilerParams(
            collective_id=0, has_side_effects=True, vmem_limit_bytes=48 * 1024 * 1024
        ),
        name="synthesis",
    )(coefficients, leaf, mix_self, mix_partner, skeleton, expand, slot_order[None, :])


def solution(mesh):
    return jax.shard_map(
        on_device,
        mesh=mesh,
        in_specs=(
            P("grp", "lat", None),
            P("grp", "lat", None),
            P("grp", None, "lat", None),
            P("grp", None, "lat", None),
            P("grp", None, "lat"),
            P("grp", "lat", None),
            P(),
        ),
        out_specs=P("grp", "lat", None),
        check_vma=False,
    )
```

time: 186 us -> 127 us (0.68)
  Pallas kernels: 0 us -> 120 us
  waiting for transfers between devices: 116 us -> 0 us
  starting transfers between devices: 33.7 us -> 0 us
  matrix products: 19.5 us -> 0 us
  blocking collectives: 12.7 us -> 0 us
  local copies, waits for them, and re-layouts: 3.61 us -> 6.52 us
    pallas_call x0 -> x1, Pallas kernels: none -> 120 us  [on_device(): pl.pallas_call(functools.partial(kernel, levels, groups, GROUP), out_shap...]
    ppermute x10 -> x0, waiting for transfers between devices: 104 us -> none  [swapped(): return lax.ppermute(value, axis, pairs)]
    ppermute x10 -> x0, starting transfers between devices: 28.2 us -> none  [swapped(): return lax.ppermute(value, axis, pairs)]
    dot_general x18 -> x0, matrix products: 19.5 us -> none  [the longest x5 4.58 us: on_device(): jnp.einsum('kac,kcs->kas', mix_self[:, level], state, preferred_element_t...]
    all_to_all x1 -> x0, blocking collectives: 12.7 us -> none  [on_device(): return lax.all_to_all(whole, 'grp', split_axis=0, concat_axis=1, tiled=True)]
    all_to_all x1 -> x0, waiting for transfers between devices: 12.1 us -> none  [on_device(): lax.all_to_all(fields, 'grp', split_axis=1, concat_axis=0, tiled=True)]
    unnamed x10, local copies, waits for them, and re-layouts: 0.02 us -> 6.52 us
    all_to_all x1 -> x0, starting transfers between devices: 5.46 us -> none  [on_device(): lax.all_to_all(fields, 'grp', split_axis=1, concat_axis=0, tiled=True)]
  transfers between devices with their start and end apart: 11 -> 0, of which waited for: 7 -> 0; matrix products, arithmetic and copies ran while one was open for 6% -> 0% of each run, Pallas kernels for 0% -> 0%
where the time goes in v1:
time: 127 us; the launch traced here: 126 us
  Pallas kernels  120 us (94%)
  local copies, waits for them, and re-layouts  6.52 us (5%)
    pallas_call x1, Pallas kernels, on_device(): pl.pallas_call(functools.partial(kernel, levels, groups, GROUP), out_shap...  120 us
    unnamed x10, local copies, waits for them, and re-layouts  6.52 us

profile of v1, /device:TPU:1, one launch (start us, length us, event | category | flops | bytes accessed | tf_op | source)
XLA Modules:
  0.0 126.3 jit_solution(11729816084217663297)
XLA Ops:
  0.0 0.8 copy.8.skel_ref
  0.9 0.0 copy-start
  0.9 1.7 %copy-done = bf16[24,128,384]{2,1,0:T(8,128)(2,1)S(1)} copy-done((bf16[24,128,384]{2,1,0:T(8,128)(2,1)S(1)}, bf16[24,128,384]{2,1,0:T(8,128)(2,1)}, u32[]{:S(2)}) %copy-start) | copy-done | bytes 2359320
  2.5 0.0 copy-start.1
  2.5 1.5 %copy-done.1 = bf16[24,5,64,128]{3,2,1,0:T(8,128)(2,1)S(1)} copy-done((bf16[24,5,64,128]{3,2,1,0:T(8,128)(2,1)S(1)}, bf16[24,5,64,128]{3,2,1,0:T(8,128)(2,1)}, u32[]{:S(2)}) %copy-start.1) | copy-done | bytes 1966104
  4.1 0.0 copy-start.2
  4.1 1.0 copy-done.2
  5.1 0.0 copy-start.3
  5.1 0.7 copy-done.3
  5.7 119.7 %synthesis.1 = bf16[32,64,128]{2,1,0:T(8,128)(2,1)S(1)} custom-call(bf16[24,384,256]{2,1,0:T(8,128)(2,1)} %coeff_h.1, bf16[24,128,384]{2,1,0:T(8,128)(2,1)S(1)} %copy-done, bf16[24,5,128,128]{3,2,1,0:T(8,128)(2,1)} %self_h.1, bf16[24,5,64,128]{3,2,1,0:T(8,128)(2,1)S(1)} %copy-done.1, s32[24,5,64]{2,1,0:T(8,128)S(1)} %copy.8.skel_ref, ...), custom_call_target="tpu_custom_call" | custom-call | tf_op jit(solution)/shard_map/synthesis/pallas_call | solution.py:235
  125.5 0.8 copy.10
Async XLA Ops:
  0.9 1.7 %copy-start = (bf16[24,128,384]{2,1,0:T(8,128)(2,1)S(1)}, bf16[24,128,384]{2,1,0:T(8,128)(2,1)}, u32[]{:S(2)}) copy-start(bf16[24,128,384]{2,1,0:T(8,128)(2,1)} %leaf_h.1) | copy-start | bytes 7077892
  2.5 1.5 %copy-start.1 = (bf16[24,5,64,128]{3,2,1,0:T(8,128)(2,1)S(1)}, bf16[24,5,64,128]{3,2,1,0:T(8,128)(2,1)}, u32[]{:S(2)}) copy-start(bf16[24,5,64,128]{3,2,1,0:T(8,128)(2,1)} %partner_h.1) | copy-start | bytes 5898244
  4.1 1.0 copy-start.2
  5.1 0.7 copy-start.3

commit v2 on v1

--- a/solution.py
+++ b/solution.py
@@ -9,7 +9,10 @@
 from jax.sharding import PartitionSpec as P
 
 LON_DEV = 32
-GROUP = 3
+GROUP = 1
+STRIDE = 2
+AHEAD = 4
+STAGES = lambda levels: range(levels + 1)
 MESH = pl.DeviceIdType.MESH
 F32 = jnp.float32
 BF16 = jnp.bfloat16
@@ -25,11 +28,11 @@
 
 def kernel(
     levels, groups, gsize,
-    coeff_h, leaf_h, self_h, partner_h, skel_ref, expand_h, order_ref, out_h,
+    coeff_h, leaf_h, self_h, partner_h, skel_h, expand_h, order_h, out_h,
     coeff_v, leaf_v, self_v, partner_v, expand_v,
-    ask_send, ask_recv, state, send_v, recv_v,
-    fields, pieces, pieces_w, whole_w, whole,
-    in_sem, ask_ssem, ask_rsem, ssem, rsem, fssem, frsem, ossem, orsem, own_sem,
+    order_v, ask_send, ask_recv, state, send_v, recv_v,
+    fields, pieces, pieces_w, whole_w, whole, cos_v, sin_v,
+    in_sem, small_sem, ask_ssem, ask_rsem, ssem, rsem, fssem, frsem, ossem, orsem, own_sem,
 ):
     slots, width = state.shape[0], state.shape[1]
     half = coeff_v.shape[2] // 2
@@ -61,15 +64,19 @@
             load(i, c).start()
         return 0
 
-    lax.fori_loop(0, chunks, start_loads, 0)
+    get_skel = pltpu.make_async_copy(skel_h, ask_send, small_sem.at[0])
+    get_order = pltpu.make_async_copy(order_h, order_v, small_sem.at[1])
+    get_skel.start()
+    get_order.start()
+    for c in range(min(AHEAD, chunks)):
+        start_loads(c, 0)
 
     barrier = pltpu.get_barrier_semaphore()
     for k in range(levels):
         pl.semaphore_signal(barrier, inc=1, device_id={"lat": partners[k]}, device_id_type=MESH)
     for other in others:
         pl.semaphore_signal(barrier, inc=1, device_id={"grp": other}, device_id_type=MESH)
-    for k in range(levels):
-        ask_send[k] = skel_ref[:, k, :]
+    get_skel.wait()
     pl.semaphore_wait(barrier, levels + groups - 1)
 
     def ask(k):
@@ -81,6 +88,17 @@
 
     for k in range(levels):
         ask(k).start()
+
+    lons = whole.shape[0]
+    total = groups * slots
+    get_order.wait()
+    order = order_v[...]
+    turn = lax.broadcasted_iota(jnp.int32, (lons, total), 0)
+    turn = (jnp.maximum(order, 0) * turn) & (lons - 1)
+    angle = 2.0 * math.pi * turn.astype(F32) / lons
+    scale = jnp.where(order >= 0, 1.0 / math.sqrt(total * 3 // 4), 0.0)
+    cos_v[...] = (jnp.cos(angle) * scale).astype(BF16)
+    sin_v[...] = (-jnp.sin(angle) * scale).astype(BF16)
 
     def exchange(k, c):
         return pltpu.make_async_remote_copy(
@@ -133,8 +151,12 @@
                 hand_over(d, c).start()
 
     def step(t, _):
-        for k in range(levels + 1):
-            c = t - k
+        @pl.when(t + AHEAD < chunks)
+        def _():
+            start_loads(t + AHEAD, 0)
+
+        for k in STAGES(levels):
+            c = t - k * STRIDE
 
             @pl.when((c >= 0) & (c < chunks))
             def _():
@@ -146,37 +168,33 @@
                 stage(k, c)
         return 0
 
-    lax.fori_loop(0, chunks + levels, step, 0)
-
-    lons = whole.shape[0]
-    total = groups * slots
-    order = order_ref[...]
-    turn = lax.broadcasted_iota(jnp.int32, (lons, total), 0)
-    turn = (jnp.maximum(order, 0) * turn) % lons
-    angle = 2.0 * math.pi * turn.astype(F32) / lons
-    scale = jnp.where(order >= 0, 1.0 / math.sqrt(total * 3 // 4), 0.0)
-    cos_table = (jnp.cos(angle) * scale).astype(BF16)
-    sin_table = (-jnp.sin(angle) * scale).astype(BF16)
-
-    pieces_w[pl.ds(grp * slots, slots)] = fields[grp].astype(F32)
+    lax.fori_loop(0, chunks + levels * STRIDE, step, 0)
+
+    def widen(block, value):
+        rows = slots * lat_part
+        flat = value.astype(F32).reshape(rows, 2 * half)
+        for part in range(2):
+            pieces_w[part, pl.ds(block * rows, rows), :] = flat[:, part * half:(part + 1) * half]
+
+    widen(grp, fields[grp])
     for d in range(groups - 1):
         pltpu.make_async_remote_copy(
             src_ref=fields.at[others[d]], dst_ref=pieces.at[senders[d]],
             send_sem=fssem.at[d], recv_sem=frsem.at[d],
             device_id={"grp": others[d]}, device_id_type=MESH,
         ).wait_recv()
-        pieces_w[pl.ds(senders[d] * slots, slots)] = pieces[senders[d]].astype(F32)
-
+        widen(senders[d], pieces[senders[d]])
+
+    cos_table, sin_table = cos_v[...], sin_v[...]
     for row in range(0, lat_part, 2):
-        cos_part, sin_part = [], []
-        for at in (row, row + 1):
-            cos_part.append(pieces_w[:, at, :half])
-            sin_part.append(pieces_w[:, at, half:])
-        mapped = dot(cos_table, jnp.concatenate(cos_part, axis=1).astype(BF16))
-        mapped = mapped + dot(sin_table, jnp.concatenate(sin_part, axis=1).astype(BF16))
-        whole_w[:, row, :] = mapped[:, :half]
-        whole_w[:, row + 1, :] = mapped[:, half:]
-    whole[...] = whole_w[...].astype(BF16)
+        parts = []
+        for part in range(2):
+            pair = [pieces_w[part, pl.ds(row + at, total, stride=lat_part), :] for at in range(2)]
+            parts.append(jnp.concatenate(pair, axis=1).astype(BF16))
+        mapped = dot(cos_table, parts[0]) + dot(sin_table, parts[1])
+        for at in range(2):
+            whole_w[pl.ds(row + at, lons, stride=lat_part), :] = mapped[:, at * half:(at + 1) * half]
+    whole[...] = whole_w[...].reshape(lons, lat_part, half).astype(BF16)
 
     lon_dev = lons // groups
 
@@ -231,11 +249,10 @@
     chunks = slots // GROUP
     dma = pltpu.SemaphoreType.DMA
     anywhere = pl.BlockSpec(memory_space=pl.ANY)
-    vmem = pl.BlockSpec(memory_space=pltpu.VMEM)
     return pl.pallas_call(
         functools.partial(kernel, levels, groups, GROUP),
         out_shape=jax.ShapeDtypeStruct((LON_DEV, lats, half), BF16),
-        in_specs=[anywhere, anywhere, anywhere, anywhere, vmem, anywhere, vmem],
+        in_specs=[anywhere] * 7,
         out_specs=anywhere,
         scratch_shapes=[
             pltpu.VMEM(coefficients.shape, BF16),
@@ -243,6 +260,7 @@
             pltpu.VMEM(mix_self.shape, BF16),
             pltpu.VMEM(mix_partner.shape, BF16),
             pltpu.VMEM(expand.shape, BF16),
+            pltpu.VMEM((1, groups * slots), jnp.int32),
             pltpu.VMEM((levels, slots, rank), jnp.int32),
             pltpu.VMEM((levels, slots, rank), jnp.int32),
             pltpu.VMEM((slots, width, columns), BF16),
@@ -250,10 +268,12 @@
             pltpu.VMEM((levels, slots, rank, columns), BF16),
             pltpu.VMEM((groups, slots, part, columns), BF16),
             pltpu.VMEM((groups, slots, part, columns), BF16),
-            pltpu.VMEM((groups * slots, part, columns), F32),
-            pltpu.VMEM((lons, part, half), F32),
+            pltpu.VMEM((2, groups * slots * part, half), F32),
+            pltpu.VMEM((lons * part, half), F32),
             pltpu.VMEM((lons, part, half), BF16),
-            dma((5, chunks)),
+            pltpu.VMEM((lons, groups * slots), BF16),
+            pltpu.VMEM((lons, groups * slots), BF16),
+            dma((5, chunks)), dma((2,)),
             dma((levels,)), dma((levels,)),
             dma((levels,)), dma((levels, chunks)),
             dma((groups - 1,)), dma((groups - 1,)),
@@ -261,10 +281,13 @@
             dma,
         ],
         compiler_params=pltpu.CompilerParams(
-            collective_id=0, has_side_effects=True, vmem_limit_bytes=48 * 1024 * 1024
+            collective_id=0, has_side_effects=True, vmem_limit_bytes=60 * 1024 * 1024
         ),
         name="synthesis",
-    )(coefficients, leaf, mix_self, mix_partner, skeleton, expand, slot_order[None, :])
+    )(
+        coefficients, leaf, mix_self, mix_partner, jnp.swapaxes(skeleton, 0, 1), expand,
+        slot_order[None, :],
+    )
 
 
 def solution(mesh):

time: 127 us -> 115 us (0.906)
  Pallas kernels: 120 us -> 113 us
  local copies, waits for them, and re-layouts: 6.52 us -> 1.87 us
    pallas_call x1, Pallas kernels: 120 us -> 113 us  [on_device(): pl.pallas_call(functools.partial(kernel, levels, groups, GROUP), out_shap...]
    unnamed x10 -> x1, local copies, waits for them, and re-layouts: 6.52 us -> 1.87 us
where the time goes in v2:
time: 115 us
  Pallas kernels  113 us (98%)
  local copies, waits for them, and re-layouts  1.87 us (2%)
    pallas_call x1, Pallas kernels, on_device(): pl.pallas_call(functools.partial(kernel, levels, groups, GROUP), out_shap...  113 us

profile of v2, /device:TPU:1, one launch (start us, length us, event | category | flops | bytes accessed | tf_op | source)
XLA Modules:
  0.0 114.6 jit_solution(11390676625814299798)
XLA Ops:
  0.0 112.7 %synthesis.1 = bf16[32,64,128]{2,1,0:T(8,128)(2,1)} custom-call(bf16[24,384,256]{2,1,0:T(8,128)(2,1)} %coeff_h.1, bf16[24,128,384]{2,1,0:T(8,128)(2,1)} %leaf_h.1, bf16[24,5,128,128]{3,2,1,0:T(8,128)(2,1)} %self_h.1, bf16[24,5,64,128]{3,2,1,0:T(8,128)(2,1)} %partner_h.1, s32[5,24,64]{2,1,0:T(8,128)} %bitcast.2, bf16[24,64,128]{2,1,0:T(8,128)(2,1)} %expand_h.1, ...), custom_call_target="tpu_custom_call" | custom-call | tf_op jit(solution)/shard_map/synthesis/pallas_call | solution.py:252
  112.7 1.9 %copy.9 = bf16[32,64,128]{2,1,0:T(8,128)(2,1)} copy(bf16[32,64,128]{2,1,0:T(8,128)(2,1)} %synthesis.1) | data formatting | bytes 1048576

commit v3 on v2

--- a/solution.py
+++ b/solution.py
@@ -10,9 +10,9 @@
 
 LON_DEV = 32
 GROUP = 1
-STRIDE = 2
+STRIDE = 3
 AHEAD = 4
-STAGES = lambda levels: range(levels + 1)
+SPLIT = 3
 MESH = pl.DeviceIdType.MESH
 F32 = jnp.float32
 BF16 = jnp.bfloat16
@@ -44,8 +44,9 @@
     for k in range(levels):
         mask = 2**k
         partners.append(lat + (1 - 2 * ((lat // mask) % 2)) * mask)
-    others = [(grp + d) % groups for d in range(1, groups)]
-    senders = [(grp + groups - d) % groups for d in range(1, groups)]
+    far = sorted(range(1, groups), key=lambda d: abs(d - groups // 2))
+    others = [(grp + d) % groups for d in far]
+    senders = [(grp + groups - d) % groups for d in far]
 
     def span(c):
         return pl.ds(c * gsize, gsize)
@@ -135,6 +136,11 @@
                 mixed = dot(self_v[q, k - 1], state[q])
                 mixed = mixed + dot_rows(partner_v[q, k - 1], recv_v[k - 1, q])
                 now = mixed.astype(BF16)
+            if k < levels and i == 0:
+                @pl.when(c == 0)
+                def _():
+                    ask(k).wait_recv()
+
             if k < levels:
                 wanted = ask_recv[k, pl.ds(q, 1), :]
                 pick = (row_of == wanted).astype(F32).astype(BF16)
@@ -150,25 +156,35 @@
             for d in range(groups - 1):
                 hand_over(d, c).start()
 
-    def step(t, _):
-        @pl.when(t + AHEAD < chunks)
+    def run(t, k):
+        c = t - k * STRIDE
+
+        @pl.when((c >= 0) & (c < chunks))
+        def _():
+            stage(k, c)
+
+    core = grp % 2
+
+    def half_step(u, _):
+        t = u // 2
+
+        @pl.when((u % 2 == 0) & (t + AHEAD < chunks))
         def _():
             start_loads(t + AHEAD, 0)
 
-        for k in STAGES(levels):
-            c = t - k * STRIDE
-
-            @pl.when((c >= 0) & (c < chunks))
-            def _():
-                if k < levels:
-                    @pl.when(c == 0)
-                    def _():
-                        ask(k).wait_recv()
-
-                stage(k, c)
+        @pl.when((u + core) % 2 == 0)
+        def _():
+            for k in range(SPLIT):
+                run(t, k)
+
+        @pl.when((u + core) % 2 == 1)
+        def _():
+            for k in range(SPLIT, levels + 1):
+                run(t, k)
+
         return 0
 
-    lax.fori_loop(0, chunks + levels * STRIDE, step, 0)
+    lax.fori_loop(0, 2 * (chunks + levels * STRIDE), half_step, 0)
 
     def widen(block, value):
         rows = slots * lat_part
@@ -252,7 +268,7 @@
     return pl.pallas_call(
         functools.partial(kernel, levels, groups, GROUP),
         out_shape=jax.ShapeDtypeStruct((LON_DEV, lats, half), BF16),
-        in_specs=[anywhere] * 7,
+        in_specs=[pl.BlockSpec(memory_space=pltpu.HBM)] * 7,
         out_specs=anywhere,
         scratch_shapes=[
             pltpu.VMEM(coefficients.shape, BF16),

time: 115 us -> 114 us (level)
  Pallas kernels: 113 us -> 111 us
    pallas_call x1, Pallas kernels: 113 us -> 111 us  [on_device(): pl.pallas_call(functools.partial(kernel, levels, groups, GROUP), out_shap...]
where the time goes in v3:
time: 114 us; the launch traced here: 113 us
  Pallas kernels  111 us (97%)
  local copies, waits for them, and re-layouts  1.87 us (2%)
    pallas_call x1, Pallas kernels, on_device(): pl.pallas_call(functools.partial(kernel, levels, groups, GROUP), out_shap...  111 us

profile of v3, /device:TPU:1, one launch (start us, length us, event | category | flops | bytes accessed | tf_op | source)
XLA Modules:
  0.0 113.4 jit_solution(486044363549400656)
XLA Ops:
  0.0 111.5 %synthesis.1 = bf16[32,64,128]{2,1,0:T(8,128)(2,1)} custom-call(bf16[24,384,256]{2,1,0:T(8,128)(2,1)} %coeff_h.1, bf16[24,128,384]{2,1,0:T(8,128)(2,1)} %leaf_h.1, bf16[24,5,128,128]{3,2,1,0:T(8,128)(2,1)} %self_h.1, bf16[24,5,64,128]{3,2,1,0:T(8,128)(2,1)} %partner_h.1, s32[5,24,64]{2,1,0:T(8,128)} %bitcast.2, bf16[24,64,128]{2,1,0:T(8,128)(2,1)} %expand_h.1, ...), custom_call_target="tpu_custom_call" | custom-call | tf_op jit(solution)/shard_map/synthesis/pallas_call | solution.py:268
  111.5 1.9 %copy.9 = bf16[32,64,128]{2,1,0:T(8,128)(2,1)} copy(bf16[32,64,128]{2,1,0:T(8,128)(2,1)} %synthesis.1) | data formatting | bytes 1048576

commit v4 on v3

--- a/solution.py
+++ b/solution.py
@@ -48,6 +48,12 @@
     others = [(grp + d) % groups for d in far]
     senders = [(grp + groups - d) % groups for d in far]
 
+    barrier = pltpu.get_barrier_semaphore()
+    for k in range(levels):
+        pl.semaphore_signal(barrier, inc=1, device_id={"lat": partners[k]}, device_id_type=MESH)
+    for other in others:
+        pl.semaphore_signal(barrier, inc=1, device_id={"grp": other}, device_id_type=MESH)
+
     def span(c):
         return pl.ds(c * gsize, gsize)
 
@@ -72,11 +78,6 @@
     for c in range(min(AHEAD, chunks)):
         start_loads(c, 0)
 
-    barrier = pltpu.get_barrier_semaphore()
-    for k in range(levels):
-        pl.semaphore_signal(barrier, inc=1, device_id={"lat": partners[k]}, device_id_type=MESH)
-    for other in others:
-        pl.semaphore_signal(barrier, inc=1, device_id={"grp": other}, device_id_type=MESH)
     get_skel.wait()
     pl.semaphore_wait(barrier, levels + groups - 1)
 

time: 114 us -> 113 us (level)
  no operation moved by 1% of the time
where the time goes in v4:
time: 113 us
  Pallas kernels  111 us (98%)
  local copies, waits for them, and re-layouts  1.87 us (2%)
    pallas_call x1, Pallas kernels, on_device(): pl.pallas_call(functools.partial(kernel, levels, groups, GROUP), out_shap...  111 us

profile of v4, /device:TPU:1, one launch (start us, length us, event | category | flops | bytes accessed | tf_op | source)
XLA Modules:
  0.0 113.3 jit_solution(37881559189020338)
XLA Ops:
  0.0 111.4 %synthesis.1 = bf16[32,64,128]{2,1,0:T(8,128)(2,1)} custom-call(bf16[24,384,256]{2,1,0:T(8,128)(2,1)} %coeff_h.1, bf16[24,128,384]{2,1,0:T(8,128)(2,1)} %leaf_h.1, bf16[24,5,128,128]{3,2,1,0:T(8,128)(2,1)} %self_h.1, bf16[24,5,64,128]{3,2,1,0:T(8,128)(2,1)} %partner_h.1, s32[5,24,64]{2,1,0:T(8,128)} %bitcast.2, bf16[24,64,128]{2,1,0:T(8,128)(2,1)} %expand_h.1, ...), custom_call_target="tpu_custom_call" | custom-call | tf_op jit(solution)/shard_map/synthesis/pallas_call | solution.py:269
  111.4 1.9 %copy.9 = bf16[32,64,128]{2,1,0:T(8,128)(2,1)} copy(bf16[32,64,128]{2,1,0:T(8,128)(2,1)} %synthesis.1) | data formatting | bytes 1048576
